TPU v7x, 256 devices: a whole 4x4x8 slice. The times are simulated.
256 devices in a mesh: sec: 2 (over core), var: 32 (over y, z), trait: 4 (over x).
Axes of the slice: x: 4, y: 4, z: 8, core: 2. Of those that a mesh axis runs over, the one named last changes fastest.
Arguments:
- z_typed: bfloat16 [262144, 512], P(('sec', 'var'), 'trait'), may hold values from -6 to 6
- band_inverse: bfloat16 [2048, 128, 384], P(('sec', 'var')), may hold values from -0.3125 to 0.3125
- ld_untyped: bfloat16 [4096, 128, 512], P(('sec', 'var')), may hold values from -0.375 to 0.375
- trait_mix: bfloat16 [512, 512], replicated, may hold values from -0.25 to 0.25
- win_start: int32 [4096], P(('sec', 'var')), may hold values from 0 to 2047, as said below
- win_count: int32 [4096], P(('sec', 'var')), may hold values from 1 to 4, as said below
Outputs:
- imputed_mixed: bfloat16 [524288, 512], P(('sec', 'var'), 'trait')
Inputs may be any that keep to these rules, and one draw needn't show every extreme that they name: Windows follow chromosome order: within the 64 untyped blocks of one index g of sec+var, win_start never falls, and every window lies in typed blocks g * 32 - 32 to (g + 1) * 32 + 31; the first window of each index starts at its lower end (or at 0) and the last one ends at its upper end (or at the chromosome's end). win_start + win_count never exceeds 2048.
All inputs are finite; a program needn't handle non-finite values.
Results may differ from a plain program's by a relative error of at most 0.0057.
Values may be sent and summed in bfloat16 or wider, within the bound.
No kernel may reach another device: no remote copies, remote signals or barrier semaphores. Data moves between devices by JAX's collectives and lax.ppermute only.
A program may use at most 64 MiB of HBM per device.

v0:
```python
import jax
import jax.numpy as jnp
from jax import lax
from jax.sharding import PartitionSpec as P

BLK = 128
WIN = 4


def padded_2(cells, sides, width):
    for axis, dim in sides:
        count = lax.axis_size(axis)
        ends = count - 1
        head = lax.slice_in_dim(cells, 0, width, axis=dim)
        tail = lax.slice_in_dim(cells, cells.shape[dim] - width, cells.shape[dim], axis=dim)
        cells = jnp.concatenate(
            [
                lax.ppermute(tail, axis, [(i, (i + 1) % count) for i in range(ends)]),
                cells,
                lax.ppermute(head, axis, [((i + 1) % count, i) for i in range(ends)]),
            ],
            axis=dim,
        )
    return cells


def on_device(z_typed, band_inverse, ld_untyped, trait_mix, win_start, win_count):
    trait_cols = z_typed.shape[1]
    typed_blocks = z_typed.shape[0] // BLK
    padded = padded_2(z_typed, ((("sec", "var"), 0),), BLK)
    stacked = jnp.concatenate(
        [
            padded[k * BLK : (k + typed_blocks) * BLK].reshape(typed_blocks, BLK, trait_cols)
            for k in range(3)
        ],
        axis=1,
    )
    whitened = jnp.einsum(
        "bij,bjc->bic", band_inverse, stacked, preferred_element_type=jnp.float32
    ).astype(jnp.bfloat16)
    whitened_rows = whitened.reshape(typed_blocks * BLK, trait_cols)
    column_start = lax.axis_index("trait") * trait_cols
    mix_cols = lax.dynamic_slice_in_dim(trait_mix, column_start, trait_cols, 1)
    mixed_sums = jnp.dot(
        lax.all_gather(whitened_rows, "trait", axis=1, tiled=True),
        mix_cols,
        preferred_element_type=jnp.float32,
    )
    mixed = mixed_sums.astype(jnp.bfloat16).reshape(typed_blocks, BLK, trait_cols)
    window_steps = jnp.arange(WIN, dtype=jnp.int32)
    usable = window_steps[None, :] < win_count[:, None]
    untyped_blocks = win_start.shape[0]
    extended = padded_2(mixed, ((("sec", "var"), 0),), typed_blocks)
    local_first = win_start - lax.axis_index(("sec", "var")) * typed_blocks + typed_blocks
    wanted = jnp.clip(local_first[:, None] + window_steps[None, :], 0, 3 * typed_blocks - 1)
    picked = extended[wanted]
    chosen = jnp.where(usable[:, :, None, None], picked, jnp.zeros_like(picked))
    window_rows = chosen.reshape(untyped_blocks, WIN * BLK, trait_cols)
    imputed = jnp.einsum(
        "uij,ujc->uic", ld_untyped, window_rows, preferred_element_type=jnp.float32
    ).astype(jnp.bfloat16)
    return imputed.reshape(untyped_blocks * BLK, trait_cols)


def solution(mesh):
    in_specs = (
        P(("sec", "var"), "trait"),
        P(("sec", "var"), None, None),
        P(("sec", "var"), None, None),
        P(),
        P(("sec", "var")),
        P(("sec", "var")),
    )
    out_specs = P(("sec", "var"), "trait")
    return jax.shard_map(
        on_device, mesh=mesh, in_specs=in_specs, out_specs=out_specs, check_vma=False
    )
```

profile of v0, /device:TPU:24, one launch (start us, length us, event | category | flops | bytes accessed | tf_op | source)
XLA Modules:
  0.0 152.1 jit_solution(10747132638285355354)
XLA Ops:
  6.5 0.0 copy-start
  6.5 0.0 all-gather.2.cloned.1.call-start
  6.5 0.9 fusion.12
  7.5 3.9 %collective-permute-start = (bf16[128,128]{1,0:T(8,128)(2,1)S(1)}, bf16[128,128]{1,0:T(8,128)(2,1)S(1)}, u32[]{:S(2)}, u32[]{:S(2)}) collective-permute-start(bf16[128,128]{1,0:T(8,128)(2,1)S(1)} %get-tuple-element.7), channel_id=1, source_target_pairs={{0,4},{4,8},{8,12},{12,16},{16,20},{20,24},{24,28},{28,32},{32,36}... | collective-permute-start | bytes 98312 | tf_op jit(solution)/shard_map/ppermute | solution.py:18
  11.4 6.0 %collective-permute-start.1 = (bf16[128,128]{1,0:T(8,128)(2,1)S(1)}, bf16[128,128]{1,0:T(8,128)(2,1)S(1)}, u32[]{:S(2)}, u32[]{:S(2)}) collective-permute-start(bf16[128,128]{1,0:T(8,128)(2,1)S(1)} %get-tuple-element.8), channel_id=1, source_target_pairs={{4,0},{8,4},{12,8},{16,12},{20,16},{24,20},{28,24},{32,28},{36,32}... | collective-permute-start | bytes 98312 | tf_op jit(solution)/shard_map/ppermute | solution.py:20
  17.5 0.0 collective-permute-done
  17.5 1.6 %collective-permute-done.1 = bf16[128,128]{1,0:T(8,128)(2,1)S(1)} collective-permute-done((bf16[128,128]{1,0:T(8,128)(2,1)S(1)}, bf16[128,128]{1,0:T(8,128)(2,1)S(1)}, u32[]{:S(2)}, u32[]{:S(2)}) %collective-permute-start.1) | collective-permute-done | bytes 32800 | tf_op jit(solution)/shard_map/ppermute | solution.py:20
  19.0 1.7 %pad_maximum_fusion.2 = (bf16[4096,128]{1,0:T(8,128)(2,1)S(1)}, bf16[4096,128]{1,0:T(8,128)(2,1)S(1)}) fusion(bf16[4096,128]{1,0:T(8,128)(2,1)} %param.6, bf16[128,128]{1,0:T(8,128)(2,1)S(1)} %collective-permute-done, bf16[128,128]{1,0:T(8,128)(2,1)S(1)} %collective-permute-done.1), kind=kLoop, calls=%fused_computation.13 | loop fusion | flops 4194304 | bytes 3211264 | tf_op jit(solution)/shard_map/concatenate | solution.py:16
  20.7 0.0 copy-done
  20.8 3.2 %fusion.6 = bf16[32,128,128]{1,2,0:T(8,128)(2,1)} fusion(bf16[32,128,384]{2,1,0:T(8,128)(2,1)S(1)} %copy-done, bf16[32,128,128]{2,1,0:T(8,128)(2,1)S(1)} %bitcast.26, bf16[32,128,128]{2,1,0:T(8,128)(2,1)} %bitcast.24, bf16[32,128,128]{2,1,0:T(8,128)(2,1)S(1)} %bitcast.25), kind=kOutput, calls=%fused_computation.11 | convolution fusion | flops 412614656 | bytes 7340032 | tf_op jit(solution)/shard_map/bij,bjc->bic/dot_general | solution.py:38
  24.0 0.0 copy-start.1
  24.0 0.0 copy-start.2
  24.0 0.0 all-gather.2.cloned.1.call-update
  24.0 55.4 %all-gather.2.cloned.1.call-done = bf16[4096,512]{1,0:T(8,128)(2,1)} async-done(((bf16[4096,128]{1,0:T(8,128)(2,1)}), bf16[4096,512]{1,0:T(8,128)(2,1)}) %all-gather.2.cloned.1.call-update) | async-done | bytes 4194320 | tf_op jit(solution)/shard_map/all_gather | solution.py:45
  79.4 4.4 %convolution_convert_fusion = bf16[4096,128]{1,0:T(8,128)(2,1)} fusion(bf16[4096,512]{1,0:T(8,128)(2,1)} %all-gather.2.cloned.1.call-done, bf16[512,512]{1,0:T(8,128)(2,1)} %param.9, s32[]{:T(128)S(6)} %select_n.18), kind=kOutput, calls=%fused_computation.2 | convolution fusion | flops 537395200 | bytes 5373956 | tf_op jit(solution)/shard_map/dot_general | solution.py:44
  83.8 5.5 %collective-permute-start.3 = (bf16[32,128,128]{2,1,0:T(8,128)(2,1)}, bf16[32,128,128]{2,1,0:T(8,128)(2,1)}, u32[]{:S(2)}, u32[]{:S(2)}) collective-permute-start(bf16[32,128,128]{2,1,0:T(8,128)(2,1)} %bitcast.5), channel_id=1, source_target_pairs={{4,0},{8,4},{12,8},{16,12},{20,16},{24,20},{28,24},{32,28},{36,32}... | collective-permute-start | bytes 3145736 | tf_op jit(solution)/shard_map/ppermute | solution.py:20
  89.3 1.9 %collective-permute-start.2 = (bf16[32,128,128]{2,1,0:T(8,128)(2,1)}, bf16[32,128,128]{2,1,0:T(8,128)(2,1)}, u32[]{:S(2)}, u32[]{:S(2)}) collective-permute-start(bf16[32,128,128]{2,1,0:T(8,128)(2,1)} %bitcast.5), channel_id=1, source_target_pairs={{0,4},{4,8},{8,12},{12,16},{16,20},{20,24},{24,28},{28,32},{32,36}... | collective-permute-start | bytes 3145736 | tf_op jit(solution)/shard_map/ppermute | solution.py:18
  91.3 0.0 copy-done.1
  91.3 0.1 iota_compare_fusion
  91.4 0.1 broadcast_in_dim.21
  91.5 0.0 copy-done.2
  91.5 0.1 compare_select_fusion
  91.6 0.1 reshape.93
  91.8 19.4 %collective-permute-done.3 = bf16[32,128,128]{2,1,0:T(8,128)(2,1)} collective-permute-done((bf16[32,128,128]{2,1,0:T(8,128)(2,1)}, bf16[32,128,128]{2,1,0:T(8,128)(2,1)}, u32[]{:S(2)}, u32[]{:S(2)}) %collective-permute-start.3) | collective-permute-done | bytes 1048608 | tf_op jit(solution)/shard_map/ppermute | solution.py:20
  111.2 6.2 %collective-permute-done.2 = bf16[32,128,128]{2,1,0:T(8,128)(2,1)} collective-permute-done((bf16[32,128,128]{2,1,0:T(8,128)(2,1)}, bf16[32,128,128]{2,1,0:T(8,128)(2,1)}, u32[]{:S(2)}, u32[]{:S(2)}) %collective-permute-start.2) | collective-permute-done | bytes 1048608 | tf_op jit(solution)/shard_map/ppermute | solution.py:18
  117.4 3.3 %pad_maximum_fusion = bf16[96,128,128]{2,1,0:T(8,128)(2,1)} fusion(bf16[32,128,128]{2,1,0:T(8,128)(2,1)} %collective-permute-done.3, bf16[32,128,128]{2,1,0:T(8,128)(2,1)} %bitcast.5, bf16[32,128,128]{2,1,0:T(8,128)(2,1)} %collective-permute-done.2), kind=kLoop, calls=%fused_computation.9 | loop fusion | flops 3145728 | bytes 6291456 | tf_op jit(solution)/shard_map/concatenate | solution.py:16
  120.7 10.5 %gather_fusion = bf16[256,128,128]{2,1,0:T(8,128)(2,1)} fusion(bf16[96,128,128]{2,1,0:T(8,128)(2,1)} %pad_maximum_fusion, s32[1024]{0:T(1024)S(1)} %pad_clamp_fusion), kind=kCustom, calls=%fused_computation | custom fusion | bytes 16778240 | tf_op jit(solution)/shard_map/gather | solution.py:56
  131.2 7.0 %bitcast_select_fusion = bf16[64,512,128]{2,1,0:T(8,128)(2,1)S(1)} fusion(pred[64,512]{1,0:T(8,128)(4,1)S(1)} %bitcast.28, bf16[64,512,128]{2,1,0:T(8,128)(2,1)} %bitcast.23), kind=kLoop, calls=%fused_computation.1 | loop fusion | flops 4194304 | bytes 16809984 | tf_op jit(solution)/shard_map/jit(_where)/select_n | solution.py:57
  138.2 7.0 %convolution_convert_fusion.1 = bf16[64,128,128]{1,2,0:T(8,128)(2,1)} fusion(bf16[64,128,512]{2,1,0:T(8,128)(2,1)} %param.8, bf16[64,512,128]{2,1,0:T(8,128)(2,1)S(1)} %bitcast_select_fusion), kind=kOutput, calls=%fused_computation.10 | convolution fusion | flops 1074790400 | bytes 18874368 | tf_op jit(solution)/shard_map/uij,ujc->uic/dot_general | solution.py:59
  (3 shorter events, 0.0 us)
Async XLA Ops:
  6.5 14.2 %copy-start = (bf16[32,128,384]{2,1,0:T(8,128)(2,1)S(1)}, bf16[32,128,384]{2,1,0:T(8,128)(2,1)}, u32[]{:S(2)}) copy-start(bf16[32,128,384]{2,1,0:T(8,128)(2,1)} %param.7) | copy-start | bytes 9437188
  6.5 72.9 %all-gather.2.cloned.1.call-start = ((), (), s32[]{:S(2)}) async-start(), calls=%async_computation | async-start | bytes 5242880 | tf_op jit(solution)/shard_map/all_gather | solution.py:45
  7.5 10.0 %collective-permute-start = (bf16[128,128]{1,0:T(8,128)(2,1)S(1)}, bf16[128,128]{1,0:T(8,128)(2,1)S(1)}, u32[]{:S(2)}, u32[]{:S(2)}) collective-permute-start(bf16[128,128]{1,0:T(8,128)(2,1)S(1)} %get-tuple-element.7), channel_id=1, source_target_pairs={{0,4},{4,8},{8,12},{12,16},{16,20},{20,24},{24,28},{28,32},{32,36}... | collective-permute-start | bytes 98312 | tf_op jit(solution)/shard_map/ppermute | solution.py:18
  11.4 7.6 %collective-permute-start.1 = (bf16[128,128]{1,0:T(8,128)(2,1)S(1)}, bf16[128,128]{1,0:T(8,128)(2,1)S(1)}, u32[]{:S(2)}, u32[]{:S(2)}) collective-permute-start(bf16[128,128]{1,0:T(8,128)(2,1)S(1)} %get-tuple-element.8), channel_id=1, source_target_pairs={{4,0},{8,4},{12,8},{16,12},{20,16},{24,20},{28,24},{32,28},{36,32}... | collective-permute-start | bytes 98312 | tf_op jit(solution)/shard_map/ppermute | solution.py:20
  24.0 67.3 %copy-start.1 = (s32[64]{0:T(128)S(1)}, s32[64]{0:T(128)}, u32[]{:S(2)}) copy-start(s32[64]{0:T(128)} %param.11) | copy-start | bytes 772
  24.0 67.5 %copy-start.2 = (s32[64]{0:T(128)S(1)}, s32[64]{0:T(128)}, u32[]{:S(2)}) copy-start(s32[64]{0:T(128)} %param.10) | copy-start | bytes 772
  83.8 27.3 %collective-permute-start.3 = (bf16[32,128,128]{2,1,0:T(8,128)(2,1)}, bf16[32,128,128]{2,1,0:T(8,128)(2,1)}, u32[]{:S(2)}, u32[]{:S(2)}) collective-permute-start(bf16[32,128,128]{2,1,0:T(8,128)(2,1)} %bitcast.5), channel_id=1, source_target_pairs={{4,0},{8,4},{12,8},{16,12},{20,16},{24,20},{28,24},{32,28},{36,32}... | collective-permute-start | bytes 3145736 | tf_op jit(solution)/shard_map/ppermute | solution.py:20
  89.3 28.1 %collective-permute-start.2 = (bf16[32,128,128]{2,1,0:T(8,128)(2,1)}, bf16[32,128,128]{2,1,0:T(8,128)(2,1)}, u32[]{:S(2)}, u32[]{:S(2)}) collective-permute-start(bf16[32,128,128]{2,1,0:T(8,128)(2,1)} %bitcast.5), channel_id=1, source_target_pairs={{0,4},{4,8},{8,12},{12,16},{16,20},{20,24},{24,28},{28,32},{32,36}... | collective-permute-start | bytes 3145736 | tf_op jit(solution)/shard_map/ppermute | solution.py:18
Sparse Core Ops, SparseCore 0:
  24.1 55.2 all-gather.1
where the time goes:
time: 152 us
  waiting for transfers between devices  82.6 us (54%)
  starting transfers between devices  17.4 us (11%)
  matrix products  14.7 us (10%)
  between operations  13.5 us (9%)
  other arithmetic  12.2 us (8%)
  local copies, waits for them, and re-layouts  11.7 us (8%)
    all_gather x1, waiting for transfers between devices, on_device(): lax.all_gather(whitened_rows, 'trait', axis=1, tiled=True)  55.4 us
    ppermute x2, waiting for transfers between devices, padded_2(): lax.ppermute(head, axis, [((i + 1) % count, i) for i in range(ends)])  21 us
    ppermute x2, starting transfers between devices, padded_2(): lax.ppermute(head, axis, [((i + 1) % count, i) for i in range(ends)])  11.5 us
    gather x1, local copies, waits for them, and re-layouts, on_device(): picked = extended[wanted]  10.5 us
    dot_general x1, matrix products, on_device(): jnp.einsum('uij,ujc->uic', ld_untyped, window_rows, preferred_element_typ...  7.04 us
    select_n x1, other arithmetic, on_device(): chosen = jnp.where(usable[:, :, None, None], picked, jnp.zeros_like(picked))  7.01 us
    ppermute x2, waiting for transfers between devices, padded_2(): lax.ppermute(tail, axis, [(i, (i + 1) % count) for i in range(ends)])  6.23 us
    ppermute x2, starting transfers between devices, padded_2(): lax.ppermute(tail, axis, [(i, (i + 1) % count) for i in range(ends)])  5.87 us
  transfers between devices with their start and end apart: 5, of which 4 were waited for; matrix products, arithmetic and copies ran while one was open for 0% of the time, Pallas kernels for 0%

commit v1 on v0

--- a/solution.py
+++ b/solution.py
@@ -41,10 +41,19 @@
     whitened_rows = whitened.reshape(typed_blocks * BLK, trait_cols)
     column_start = lax.axis_index("trait") * trait_cols
     mix_cols = lax.dynamic_slice_in_dim(trait_mix, column_start, trait_cols, 1)
+
+    def _attach_rates(vector, device_axis):
+        item_now = lax.all_to_all(
+            jnp.stack([vector for _ in range(lax.axis_size(device_axis))], axis=0),
+            device_axis,
+            0,
+            0,
+        )
+        y1 = jnp.concatenate(item_now, axis=1)
+        return y1
+
     mixed_sums = jnp.dot(
-        lax.all_gather(whitened_rows, "trait", axis=1, tiled=True),
-        mix_cols,
-        preferred_element_type=jnp.float32,
+        _attach_rates(whitened_rows, "trait"), mix_cols, preferred_element_type=jnp.float32
     )
     mixed = mixed_sums.astype(jnp.bfloat16).reshape(typed_blocks, BLK, trait_cols)
     window_steps = jnp.arange(WIN, dtype=jnp.int32)

time: 152 us -> 142 us (0.934)
  between operations: 13.5 us -> 0.16 us
  waiting for transfers between devices: 82.6 us -> 74.3 us
  local copies, waits for them, and re-layouts: 11.7 us -> 17.7 us
  starting transfers between devices: 17.4 us -> 22.8 us
    all_gather x1 -> x0, waiting for transfers between devices: 55.4 us -> none  [on_device(): lax.all_gather(whitened_rows, 'trait', axis=1, tiled=True)]
    all_to_all x0 -> x1, waiting for transfers between devices: none -> 48.3 us  [_attach_rates(): lax.all_to_all(jnp.stack([vector for _ in range(lax.axis_size(device_axis...]
    another operation x0 -> x2, local copies, waits for them, and re-layouts: none -> 5.97 us  [_attach_rates(): jnp.stack([vector for _ in range(lax.axis_size(device_axis))], axis=0)]
    all_to_all x0 -> x1, starting transfers between devices: none -> 4.83 us  [_attach_rates(): lax.all_to_all(jnp.stack([vector for _ in range(lax.axis_size(device_axis...]
where the time goes in v1:
time: 142 us
  waiting for transfers between devices  74.3 us (52%)
  starting transfers between devices  22.8 us (16%)
  local copies, waits for them, and re-layouts  17.7 us (12%)
  matrix products  14.7 us (10%)
  other arithmetic  12.1 us (9%)
    all_to_all x1, waiting for transfers between devices, _attach_rates(): lax.all_to_all(jnp.stack([vector for _ in range(lax.axis_size(device_axis...  48.3 us
    ppermute x2, waiting for transfers between devices, padded_2(): lax.ppermute(head, axis, [((i + 1) % count, i) for i in range(ends)])  19.8 us
    ppermute x2, starting transfers between devices, padded_2(): lax.ppermute(head, axis, [((i + 1) % count, i) for i in range(ends)])  12.1 us
    gather x1, local copies, waits for them, and re-layouts, on_device(): picked = extended[wanted]  10.5 us
    dot_general x1, matrix products, on_device(): jnp.einsum('uij,ujc->uic', ld_untyped, window_rows, preferred_element_typ...  7.04 us
    select_n x1, other arithmetic, on_device(): chosen = jnp.where(usable[:, :, None, None], picked, jnp.zeros_like(picked))  7.01 us
    ppermute x2, waiting for transfers between devices, padded_2(): lax.ppermute(tail, axis, [(i, (i + 1) % count) for i in range(ends)])  6.23 us
    another operation x2, local copies, waits for them, and re-layouts, _attach_rates(): jnp.stack([vector for _ in range(lax.axis_size(device_axis))], axis=0)  5.97 us
  transfers between devices with their start and end apart: 5, of which 4 were waited for; matrix products, arithmetic and copies ran while one was open for 0% of the time, Pallas kernels for 0%

profile of v1, /device:TPU:24, one launch (start us, length us, event | category | flops | bytes accessed | tf_op | source)
XLA Modules:
  0.0 141.8 jit_solution(6393637339086089391)
XLA Ops:
  0.0 0.0 copy-start
  0.0 0.9 fusion.12
  0.9 3.9 %collective-permute-start = (bf16[128,128]{1,0:T(8,128)(2,1)S(1)}, bf16[128,128]{1,0:T(8,128)(2,1)S(1)}, u32[]{:S(2)}, u32[]{:S(2)}) collective-permute-start(bf16[128,128]{1,0:T(8,128)(2,1)S(1)} %get-tuple-element.7), channel_id=1, source_target_pairs={{0,4},{4,8},{8,12},{12,16},{16,20},{20,24},{24,28},{28,32},{32,36}... | collective-permute-start | bytes 98312 | tf_op jit(solution)/shard_map/ppermute | solution.py:18
  4.9 6.0 %collective-permute-start.1 = (bf16[128,128]{1,0:T(8,128)(2,1)S(1)}, bf16[128,128]{1,0:T(8,128)(2,1)S(1)}, u32[]{:S(2)}, u32[]{:S(2)}) collective-permute-start(bf16[128,128]{1,0:T(8,128)(2,1)S(1)} %get-tuple-element.8), channel_id=1, source_target_pairs={{4,0},{8,4},{12,8},{16,12},{20,16},{24,20},{28,24},{32,28},{36,32}... | collective-permute-start | bytes 98312 | tf_op jit(solution)/shard_map/ppermute | solution.py:20
  10.9 0.0 collective-permute-done
  10.9 1.6 %collective-permute-done.1 = bf16[128,128]{1,0:T(8,128)(2,1)S(1)} collective-permute-done((bf16[128,128]{1,0:T(8,128)(2,1)S(1)}, bf16[128,128]{1,0:T(8,128)(2,1)S(1)}, u32[]{:S(2)}, u32[]{:S(2)}) %collective-permute-start.1) | collective-permute-done | bytes 32800 | tf_op jit(solution)/shard_map/ppermute | solution.py:20
  12.5 1.7 %pad_maximum_fusion.2 = (bf16[4096,128]{1,0:T(8,128)(2,1)S(1)}, bf16[4096,128]{1,0:T(8,128)(2,1)S(1)}) fusion(bf16[4096,128]{1,0:T(8,128)(2,1)} %param.6, bf16[128,128]{1,0:T(8,128)(2,1)S(1)} %collective-permute-done, bf16[128,128]{1,0:T(8,128)(2,1)S(1)} %collective-permute-done.1), kind=kLoop, calls=%fused_computation.13 | loop fusion | flops 4194304 | bytes 3211264 | tf_op jit(solution)/shard_map/concatenate | solution.py:16
  14.2 0.0 copy-done
  14.2 3.2 %fusion.6 = bf16[32,128,128]{1,2,0:T(8,128)(2,1)} fusion(bf16[32,128,384]{2,1,0:T(8,128)(2,1)S(1)} %copy-done, bf16[32,128,128]{2,1,0:T(8,128)(2,1)S(1)} %bitcast.29, bf16[32,128,128]{2,1,0:T(8,128)(2,1)} %bitcast.27, bf16[32,128,128]{2,1,0:T(8,128)(2,1)S(1)} %bitcast.28), kind=kOutput, calls=%fused_computation.11 | convolution fusion | flops 412614656 | bytes 7340032 | tf_op jit(solution)/shard_map/bij,bjc->bic/dot_general | solution.py:38
  17.4 2.3 %copy.7 = bf16[4096,128]{0,1:T(8,128)(2,1)} copy(bf16[4096,128]{1,0:T(8,128)(2,1)} %bitcast.30) | data formatting | bytes 2097152 | tf_op jit(solution)/shard_map/stack;reshape | solution.py:47
  19.7 3.7 %stack.3 = bf16[4,4096,128]{1,2,0:T(8,128)(2,1)} broadcast(bf16[4096,128]{0,1:T(8,128)(2,1)} %copy.7), dimensions={1,2} | broadcast | bytes 5242880 | tf_op jit(solution)/shard_map/stack | solution.py:47
  23.4 4.8 %all-to-all-start = ((bf16[4,4096,128]{1,2,0:T(8,128)(2,1)}), bf16[4,4096,128]{1,2,0:T(8,128)(2,1)}, u32[]{:S(2)}, u32[]{:S(2)}) async-start(bf16[4,4096,128]{1,2,0:T(8,128)(2,1)} %stack.3), calls=%async_computation | async-start | bytes 8388608 | tf_op jit(solution)/shard_map/all_to_all | solution.py:46
  28.2 0.0 copy-start.1
  28.3 0.0 copy-start.2
  28.3 48.3 %all-to-all-done = bf16[4,4096,128]{1,2,0:T(8,128)(2,1)} async-done(((bf16[4,4096,128]{1,2,0:T(8,128)(2,1)}), bf16[4,4096,128]{1,2,0:T(8,128)(2,1)}, u32[]{:S(2)}, u32[]{:S(2)}) %all-to-all-start) | async-done | bytes 4194336 | tf_op jit(solution)/shard_map/all_to_all | solution.py:46
  76.5 4.5 %convolution_convert_fusion = bf16[4096,128]{1,0:T(8,128)(2,1)} fusion(bf16[4096,512]{0,1:T(8,128)(2,1)} %bitcast.6, bf16[512,512]{1,0:T(8,128)(2,1)} %param.9, s32[]{:T(128)S(6)} %select_n.18), kind=kOutput, calls=%fused_computation.2 | convolution fusion | flops 537395200 | bytes 5373956 | tf_op jit(solution)/shard_map/dot_general | solution.py:55
  81.0 6.0 %collective-permute-start.3 = (bf16[32,128,128]{2,1,0:T(8,128)(2,1)}, bf16[32,128,128]{2,1,0:T(8,128)(2,1)}, u32[]{:S(2)}, u32[]{:S(2)}) collective-permute-start(bf16[32,128,128]{2,1,0:T(8,128)(2,1)} %bitcast.7), channel_id=1, source_target_pairs={{4,0},{8,4},{12,8},{16,12},{20,16},{24,20},{28,24},{32,28},{36,32}... | collective-permute-start | bytes 3145736 | tf_op jit(solution)/shard_map/ppermute | solution.py:20
  87.0 1.9 %collective-permute-start.2 = (bf16[32,128,128]{2,1,0:T(8,128)(2,1)}, bf16[32,128,128]{2,1,0:T(8,128)(2,1)}, u32[]{:S(2)}, u32[]{:S(2)}) collective-permute-start(bf16[32,128,128]{2,1,0:T(8,128)(2,1)} %bitcast.7), channel_id=1, source_target_pairs={{0,4},{4,8},{8,12},{12,16},{16,20},{20,24},{24,28},{28,32},{32,36}... | collective-permute-start | bytes 3145736 | tf_op jit(solution)/shard_map/ppermute | solution.py:18
  89.0 0.0 copy-done.1
  89.0 0.1 iota_compare_fusion
  89.1 0.1 broadcast_in_dim.21
  89.2 0.0 copy-done.2
  89.3 0.1 compare_select_fusion
  89.3 0.1 reshape.99
  89.5 18.2 %collective-permute-done.3 = bf16[32,128,128]{2,1,0:T(8,128)(2,1)} collective-permute-done((bf16[32,128,128]{2,1,0:T(8,128)(2,1)}, bf16[32,128,128]{2,1,0:T(8,128)(2,1)}, u32[]{:S(2)}, u32[]{:S(2)}) %collective-permute-start.3) | collective-permute-done | bytes 1048608 | tf_op jit(solution)/shard_map/ppermute | solution.py:20
  107.7 6.2 %collective-permute-done.2 = bf16[32,128,128]{2,1,0:T(8,128)(2,1)} collective-permute-done((bf16[32,128,128]{2,1,0:T(8,128)(2,1)}, bf16[32,128,128]{2,1,0:T(8,128)(2,1)}, u32[]{:S(2)}, u32[]{:S(2)}) %collective-permute-start.2) | collective-permute-done | bytes 1048608 | tf_op jit(solution)/shard_map/ppermute | solution.py:18
  113.9 3.3 %pad_maximum_fusion = bf16[96,128,128]{2,1,0:T(8,128)(2,1)} fusion(bf16[32,128,128]{2,1,0:T(8,128)(2,1)} %collective-permute-done.3, bf16[32,128,128]{2,1,0:T(8,128)(2,1)} %bitcast.7, bf16[32,128,128]{2,1,0:T(8,128)(2,1)} %collective-permute-done.2), kind=kLoop, calls=%fused_computation.9 | loop fusion | flops 3145728 | bytes 6291456 | tf_op jit(solution)/shard_map/concatenate | solution.py:16
  117.2 10.5 %gather_fusion = bf16[256,128,128]{2,1,0:T(8,128)(2,1)} fusion(bf16[96,128,128]{2,1,0:T(8,128)(2,1)} %pad_maximum_fusion, s32[1024]{0:T(1024)S(1)} %pad_clamp_fusion), kind=kCustom, calls=%fused_computation | custom fusion | bytes 16778240 | tf_op jit(solution)/shard_map/gather | solution.py:65
  127.7 7.0 %bitcast_select_fusion = bf16[64,512,128]{2,1,0:T(8,128)(2,1)S(1)} fusion(pred[64,512]{1,0:T(8,128)(4,1)S(1)} %bitcast.31, bf16[64,512,128]{2,1,0:T(8,128)(2,1)} %bitcast.26), kind=kLoop, calls=%fused_computation.1 | loop fusion | flops 4194304 | bytes 16809984 | tf_op jit(solution)/shard_map/jit(_where)/select_n | solution.py:66
  134.7 7.0 %convolution_convert_fusion.1 = bf16[64,128,128]{1,2,0:T(8,128)(2,1)} fusion(bf16[64,128,512]{2,1,0:T(8,128)(2,1)} %param.8, bf16[64,512,128]{2,1,0:T(8,128)(2,1)S(1)} %bitcast_select_fusion), kind=kOutput, calls=%fused_computation.10 | convolution fusion | flops 1074790400 | bytes 18874368 | tf_op jit(solution)/shard_map/uij,ujc->uic/dot_general | solution.py:68
  (3 shorter events, 0.0 us)
Async XLA Ops:
  0.0 14.2 %copy-start = (bf16[32,128,384]{2,1,0:T(8,128)(2,1)S(1)}, bf16[32,128,384]{2,1,0:T(8,128)(2,1)}, u32[]{:S(2)}) copy-start(bf16[32,128,384]{2,1,0:T(8,128)(2,1)} %param.7) | copy-start | bytes 9437188
  0.9 10.0 %collective-permute-start = (bf16[128,128]{1,0:T(8,128)(2,1)S(1)}, bf16[128,128]{1,0:T(8,128)(2,1)S(1)}, u32[]{:S(2)}, u32[]{:S(2)}) collective-permute-start(bf16[128,128]{1,0:T(8,128)(2,1)S(1)} %get-tuple-element.7), channel_id=1, source_target_pairs={{0,4},{4,8},{8,12},{12,16},{16,20},{20,24},{24,28},{28,32},{32,36}... | collective-permute-start | bytes 98312 | tf_op jit(solution)/shard_map/ppermute | solution.py:18
  4.9 7.6 %collective-permute-start.1 = (bf16[128,128]{1,0:T(8,128)(2,1)S(1)}, bf16[128,128]{1,0:T(8,128)(2,1)S(1)}, u32[]{:S(2)}, u32[]{:S(2)}) collective-permute-start(bf16[128,128]{1,0:T(8,128)(2,1)S(1)} %get-tuple-element.8), channel_id=1, source_target_pairs={{4,0},{8,4},{12,8},{16,12},{20,16},{24,20},{28,24},{32,28},{36,32}... | collective-permute-start | bytes 98312 | tf_op jit(solution)/shard_map/ppermute | solution.py:20
  23.4 53.1 %all-to-all-start = ((bf16[4,4096,128]{1,2,0:T(8,128)(2,1)}), bf16[4,4096,128]{1,2,0:T(8,128)(2,1)}, u32[]{:S(2)}, u32[]{:S(2)}) async-start(bf16[4,4096,128]{1,2,0:T(8,128)(2,1)} %stack.3), calls=%async_computation | async-start | bytes 8388608 | tf_op jit(solution)/shard_map/all_to_all | solution.py:46
  28.2 60.7 %copy-start.1 = (s32[64]{0:T(128)S(1)}, s32[64]{0:T(128)}, u32[]{:S(2)}) copy-start(s32[64]{0:T(128)} %param.11) | copy-start | bytes 772
  28.3 61.0 %copy-start.2 = (s32[64]{0:T(128)S(1)}, s32[64]{0:T(128)}, u32[]{:S(2)}) copy-start(s32[64]{0:T(128)} %param.10) | copy-start | bytes 772
  81.0 26.7 %collective-permute-start.3 = (bf16[32,128,128]{2,1,0:T(8,128)(2,1)}, bf16[32,128,128]{2,1,0:T(8,128)(2,1)}, u32[]{:S(2)}, u32[]{:S(2)}) collective-permute-start(bf16[32,128,128]{2,1,0:T(8,128)(2,1)} %bitcast.7), channel_id=1, source_target_pairs={{4,0},{8,4},{12,8},{16,12},{20,16},{24,20},{28,24},{32,28},{36,32}... | collective-permute-start | bytes 3145736 | tf_op jit(solution)/shard_map/ppermute | solution.py:20
  87.0 26.9 %collective-permute-start.2 = (bf16[32,128,128]{2,1,0:T(8,128)(2,1)}, bf16[32,128,128]{2,1,0:T(8,128)(2,1)}, u32[]{:S(2)}, u32[]{:S(2)}) collective-permute-start(bf16[32,128,128]{2,1,0:T(8,128)(2,1)} %bitcast.7), channel_id=1, source_target_pairs={{0,4},{4,8},{8,12},{12,16},{16,20},{20,24},{24,28},{28,32},{32,36}... | collective-permute-start | bytes 3145736 | tf_op jit(solution)/shard_map/ppermute | solution.py:18
